TPU v7x, 32 devices: a whole 2x2x4 slice. The times are simulated.
32 devices in a mesh: dir: 8 (over y, x, core), freq: 4 (over z).
Axes of the slice: x: 2, y: 2, z: 4, core: 2. Of those that a mesh axis runs over, the one named last changes fastest.
Arguments:
- observed: float32 [512, 8, 2, 2, 512], P('dir', 'freq'), as said below
- flags: int32 [512, 2, 512], P('dir'), may hold values from 0 to 1, as said below
- screen: float32 [16, 512], P('dir'), may hold values from -6 to 6
- screen_kernel: float32 [512, 512], replicated
- station_uv: float32 [2, 2, 512], replicated, may hold values from -360 to 360
- source_lm: float32 [2, 3072], P(None, 'dir'), may hold values from -0.05 to 0.05
- source_flux: float32 [3072], P('dir')
- station_gain: bfloat16 [8, 2, 2, 512, 3072], P('freq', None, None, None, 'dir'), may hold values from -4.1875 to 4.1875
- source_direction: int32 [3072], P('dir'), may hold values from 0 to 1
- freq_ratio: float32 [8], P('freq')
Outputs:
- residual: float32 [512, 8, 2, 2, 512], P('dir', 'freq')
- updated_screen: float32 [16, 512], P('dir')
Inputs may be any that keep to these rules, and one draw needn't show every extreme that they name: observed is Hermitian in its stations: observed[p, f, t, 0, q] equals observed[q, f, t, 0, p] and observed[p, f, t, 1, q] equals minus observed[q, f, t, 1, p]. flags[p, t, q] equals flags[q, t, p].
All inputs are finite; a program needn't handle non-finite values.
Results may differ from a plain program's by a relative error of at most 0.0037.
Values may be sent and summed in bfloat16 or wider, within the bound.
A program may use at most 128 MiB of HBM per device.

v0:
```python
import math
import jax
import jax.numpy as jnp
from jax import lax
from jax.sharding import PartitionSpec as P

step_size = 0.3
epsilon = 1e-06
highest = lax.Precision.HIGHEST


def body(
    observed,
    flags,
    screen,
    screen_kernel,
    station_uv,
    source_lm,
    source_flux,
    station_gain,
    source_direction,
    freq_ratio,
):
    dir_count = lax.axis_size("dir")
    stations = screen.shape[1]
    local_dirs = screen.shape[0]
    local_sources = source_flux.shape[0]
    local_rows = observed.shape[0]
    channels = freq_ratio.shape[0]
    times_count = station_uv.shape[0]
    matrices = channels * times_count
    scaling = 1.0 / math.sqrt(local_sources * dir_count)
    onehot_dirs = (
        source_direction[:, None] == jnp.arange(local_dirs, dtype=jnp.int32)[None, :]
    ).astype(jnp.float32)
    screen_src = jnp.einsum("dp,kd->pk", screen, onehot_dirs, precision=highest)
    freq_each = jnp.repeat(freq_ratio, times_count)
    uv_each = jnp.tile(station_uv, (channels, 1, 1))
    geometry = jnp.einsum("mcp,ck->pmk", uv_each, source_lm, precision=highest)
    phase_angle = (
        screen_src[:, None, :] / freq_each[None, :, None]
        + (2.0 * math.pi * freq_each)[None, :, None] * geometry
    )
    gain_all = station_gain.reshape(matrices, 2, stations, local_sources).astype(jnp.float32)
    gain_re = jnp.transpose(gain_all[:, 0], (1, 0, 2))
    gain_im = jnp.transpose(gain_all[:, 1], (1, 0, 2))
    cosine = jnp.cos(phase_angle)
    sine = jnp.sin(phase_angle)
    amplitude = jnp.sqrt(source_flux)[None, None, :]
    phasor_re = (amplitude * (gain_re * cosine - gain_im * sine)).astype(jnp.bfloat16)
    phasor_im = (amplitude * (gain_re * sine + gain_im * cosine)).astype(jnp.bfloat16)
    left_mat = jnp.concatenate([phasor_re, phasor_im], axis=2)
    skew_mat = jnp.concatenate([phasor_im, -phasor_re], axis=2)
    real_part = jnp.einsum("pmk,qmk->pmq", left_mat, left_mat, preferred_element_type=jnp.float32)
    imag_part = jnp.einsum("pmk,qmk->pmq", skew_mat, left_mat, preferred_element_type=jnp.float32)
    packed_rows = lax.psum_scatter(
        (real_part + imag_part) * scaling, "dir", scatter_dimension=0, tiled=True
    )
    mirrored = lax.all_to_all(packed_rows, "dir", split_axis=2, concat_axis=0, tiled=True)
    mirrored = jnp.transpose(mirrored, (2, 1, 0))
    model_rows = jnp.stack([(packed_rows + mirrored) * 0.5, (packed_rows - mirrored) * 0.5], axis=2)
    row_ids = lax.axis_index("dir") * local_rows + jnp.arange(local_rows, dtype=jnp.int32)
    cross_baseline = (row_ids[:, None] != jnp.arange(stations, dtype=jnp.int32)[None, :]).astype(
        jnp.float32
    )
    baseline_keep = (
        jnp.tile(flags, (1, channels, 1)).astype(jnp.float32) * cross_baseline[:, None, :]
    )
    obs_rows = observed.reshape(local_rows, matrices, 2, stations)
    residual = baseline_keep[:, :, None, :] * (obs_rows - model_rows)
    resid_half = residual.astype(jnp.bfloat16)
    forward_mat = jnp.stack([left_mat, -skew_mat], axis=2)
    conj_mat = jnp.concatenate([phasor_re, -phasor_im], axis=2)
    dual_mat = jnp.concatenate([phasor_im, phasor_re], axis=2)
    adjoint_mat = jnp.stack([conj_mat, dual_mat], axis=2)
    rows_piece = lax.all_gather(resid_half, "dir", axis=0, tiled=True)
    row_part = jnp.einsum(
        "rmwq,qmwk->rmk", rows_piece, forward_mat, preferred_element_type=jnp.float32
    )
    col_total = jnp.einsum(
        "rmwp,rmwk->pmk", rows_piece, adjoint_mat, preferred_element_type=jnp.float32
    )
    weight_re = row_part[..., :local_sources] + col_total[..., :local_sources]
    weight_im = row_part[..., local_sources:] - col_total[..., local_sources:]
    source_grad = (
        phasor_im.astype(jnp.float32) * weight_re - phasor_re.astype(jnp.float32) * weight_im
    )
    source_grad = source_grad * (scaling / freq_each)[None, :, None]
    local_grad = jnp.einsum("pmk,kd->dp", source_grad, onehot_dirs, precision=highest)
    entry_count = local_dirs * dir_count * stations
    total_grad = lax.psum(local_grad, "freq")
    smooth = jnp.dot(total_grad, screen_kernel, precision=highest)
    total_sq = lax.psum(jnp.sum(smooth * smooth), "dir")
    updated = screen - step_size * smooth * lax.rsqrt(total_sq / entry_count + epsilon)
    return (residual.reshape(observed.shape), updated)


def solution(mesh):
    placed = (
        P("dir", "freq", None, None, None),
        P("dir", None, None),
        P("dir", None),
        P(),
        P(),
        P(None, "dir"),
        P("dir"),
        P("freq", None, None, None, "dir"),
        P("dir"),
        P("freq"),
    )
    return jax.shard_map(
        body,
        mesh=mesh,
        in_specs=placed,
        out_specs=(P("dir", "freq", None, None, None), P("dir", None)),
        check_vma=False,
    )
```

profile of v0, /device:TPU:0, one launch (start us, length us, event | category | flops | bytes accessed | tf_op | source)
XLA Modules:
  0.0 248.1 jit_solution(14236749292300200952)
XLA Ops:
  8.8 5.5 %copy.27 = f32[2,2,2,512,384]{3,4,1,0,2:T(8,128)} copy(bf16[2,2,2,512,384]{4,3,2,1,0:T(8,128)(2,1)} %param.17) | data formatting | bytes 9437184 | tf_op jit(solution)/shard_map/convert_element_type | solution.py:44
  14.9 14.2 %fusion.46 = (f32[512,4,384]{0,2,1:T(8,128)S(1)}, f32[512,4,384]{0,2,1:T(8,128)S(1)}) fusion(f32[4,2,512]{2,1,0:T(2,128)S(1)} %bitcast.86, f32[2,384]{1,0:T(2,128)S(1)} %copy-done.12, f32[4]{0:T(128)S(1)} %get-tuple-element.16, f32[4]{0:T(128)S(1)} %div.26, f32[512,384]{0,1:T(8,128)S(1)} %convolution_bitcast_fusion), kind=kOutput, calls=%fused_computation.68 | convolution fusion | flops 21233664 | bytes 7097376 | tf_op jit(solution)/shard_map/mcp,ck->pmk/dot_general | solution.py:39
  29.1 3.2 %fusion.45 = (bf16[512,4,384]{0,2,1:T(8,128)(2,1)}, bf16[512,4,384]{0,2,1:T(8,128)(2,1)S(1)}, bf16[512,4,1,384]{0,3,1,2:T(8,128)(2,1)}, bf16[512,4,384]{0,2,1:T(8,128)(2,1)S(1)}) fusion(f32[512,4,384]{0,2,1:T(8,128)S(1)} %get-tuple-element.10, f32[4,2,512,384]{2,3,0,1:T(8,128)S(1)} %bitcast.78, f32[512,4,384]{0,2,1:T(8,128)S(1)} %get-tuple-element.11, ...), kind=kLoop, calls=%fused_computation.67 | loop fusion | flops 9437184 | bytes 18875904 | tf_op jit(solution)/shard_map/neg | solution.py:73
  32.6 2.1 fusion.30
  34.7 3.5 %multiply_bitcast_fusion = f32[512,4,512]{0,2,1:T(8,128)} fusion(f32[4,512,512]{2,1,0:T(8,128)S(1)} %fusion.30, bf16[512,4,384]{0,2,1:T(8,128)(2,1)S(1)} %get-tuple-element.5, bf16[512,4,384]{0,2,1:T(8,128)(2,1)S(1)} %neg.16, bf16[512,4,384]{0,2,1:T(8,128)(2,1)S(1)} %get-tuple-element.7), kind=kOutput, calls=%fused_computation.8 | convolution fusion | flops 1625292800 | bytes 13107200 | tf_op jit(solution)/shard_map/pmk,qmk->pmq/dot_general | solution.py:55
  38.1 5.5 %copy.32 = f32[512,4,512]{2,1,0:T(4,128)} copy(f32[512,4,512]{0,2,1:T(8,128)} %multiply_bitcast_fusion) | data formatting | bytes 8388608 | tf_op jit(solution)/shard_map/mul | solution.py:57
  44.8 1.3 convert_element_type.49
  47.3 80.0 %all-reduce.3.cloned.1.call-done = f32[512,4,512]{2,1,0:T(4,128)} async-done(((f32[512,4,512]{2,1,0:T(4,128)}), f32[512,4,512]{2,1,0:T(4,128)}) %all-reduce.3.cloned.1.call-update) | async-done | bytes 4194320
  127.3 1.1 constant_dynamic-slice_fusion
  128.4 1.3 copy.33
  129.7 3.0 %reshape.106 = f32[8,1,16384]{2,1,0:T(1,128)} reshape(f32[512,4,64]{2,1,0:T(4,128)} %bitcast.83) | data formatting | bytes 1048576
  132.7 3.5 %all-to-all-start = ((f32[8,1,16384]{2,1,0:T(1,128)}), f32[8,1,16384]{2,1,0:T(1,128)S(1)}, u32[]{:S(2)}, u32[]{:S(2)}) async-start(f32[8,1,16384]{2,1,0:T(1,128)} %reshape.106), calls=%async_computation | async-start | bytes 1048576 | tf_op jit(solution)/shard_map/all_to_all | solution.py:59
  136.5 2.0 broadcast_multiply_fusion
  138.5 7.4 %all-to-all-done = f32[8,1,16384]{2,1,0:T(1,128)S(1)} async-done(((f32[8,1,16384]{2,1,0:T(1,128)}), f32[8,1,16384]{2,1,0:T(1,128)S(1)}, u32[]{:S(2)}, u32[]{:S(2)}) %all-to-all-start) | async-done | bytes 524320 | tf_op jit(solution)/shard_map/all_to_all | solution.py:59
  147.2 2.9 %reduce = f32[8,16384]{1,0:T(8,128)S(1)} reduce(f32[8,1,16384]{2,1,0:T(1,128)} %copy-done.7, f32[]{:T(128)} %broadcast.60), dimensions={1}, to_apply=%all_to_all.13.reduce_sub_computation | reduce | bytes 1048580 | tf_op jit(solution)/shard_map/all_to_all | solution.py:59
  150.1 1.7 reshape.107
  151.8 2.8 %copy.64 = f32[64,4,8,64]{0,2,1,3:T(8,128)} copy(f32[64,4,8,64]{0,1,3,2:T(4,128)} %bitcast.84) | data formatting | bytes 1048576 | tf_op jit(solution)/shard_map/all_to_all | solution.py:59
  154.6 2.4 all_to_all.16
  156.9 1.4 fusion.34
  159.2 1.8 fusion.33
  162.0 4.4 %maximum_negate_fusion = bf16[512,4,1,768]{0,3,1,2:T(8,128)(2,1)} fusion(bf16[512,4,1,384]{0,3,1,2:T(8,128)(2,1)} %get-tuple-element.6, bf16[512,4,1,384]{0,3,1,2:T(8,128)(2,1)} %bitcast.79), kind=kLoop, calls=%fused_computation.29 | loop fusion | flops 7864320 | bytes 6291456 | tf_op jit(solution)/shard_map/neg | solution.py:72
  167.3 3.8 %fusion.29 = (bf16[512,4,1,768]{0,3,1,2:T(8,128)(2,1)}, bf16[512,4,1,768]{0,3,1,2:T(8,128)(2,1)}, bf16[512,4,1,768]{0,3,1,2:T(8,128)(2,1)}) fusion(bf16[512,4,384]{0,2,1:T(8,128)(2,1)S(1)} %copy-done.2, bf16[512,4,384]{0,2,1:T(8,128)(2,1)S(1)} %get-tuple-element.7, bf16[512,4,384]{0,2,1:T(8,128)(2,1)S(1)} %copy-done.4), kind=kLoop, calls=%fused_computation.34 | loop fusion | flops 17301504 | bytes 14155776 | tf_op jit(solution)/shard_map/stack | solution.py:72
  171.1 2.6 %stack.42 = f32[64,2,2,1,512]{4,3,2,1,0:T(1,128)} reshape(f32[64,4,512]{2,1,0:T(4,128)} %copy-done.5) | data formatting | bytes 1048576 | tf_op jit(solution)/shard_map/stack | solution.py:61
  173.7 1.5 stack.43
  175.2 3.9 %fusion.31 = f32[64,2,2,2,512]{4,3,2,1,0:T(2,128)} fusion(f32[64,2,2,2,512]{4,3,2,1,0:T(2,128)} %param.10, f32[64,2,2,1,512]{4,3,2,1,0:T(1,128)} %stack.43, f32[64,2,2,1,512]{4,3,2,1,0:T(1,128)} %stack.42, f32[64,2,2,512]{3,2,1,0:T(2,128)} %broadcast_multiply_fusion.1), kind=kLoop, calls=%fused_computation.38 | loop fusion | flops 786432 | bytes 3670016 | tf_op jit(solution)/shard_map/mul | solution.py:70
  179.1 18.7 %all-gather.2.cloned.1.call-done = bf16[512,4,2,512]{3,1,2,0:T(4,128)(2,1)} async-done(((bf16[64,4,2,512]{3,1,2,0:T(4,128)(2,1)}), bf16[512,4,2,512]{3,1,2,0:T(4,128)(2,1)}) %all-gather.2.cloned.1.call-update) | async-done | bytes 4194320 | tf_op jit(solution)/shard_map/all_gather | solution.py:76
  197.8 7.7 %fusion.24 = f32[512,4,768]{0,2,1:T(8,128)S(1)} fusion(bf16[512,4,2,512]{3,1,2,0:T(4,128)(2,1)} %all-gather.2.cloned.1.call-done, bf16[512,4,1,768]{0,3,1,2:T(8,128)(2,1)} %maximum_negate_fusion, bf16[512,4,1,768]{0,3,1,2:T(8,128)(2,1)} %get-tuple-element.8), kind=kOutput, calls=%fused_computation.33 | convolution fusion | flops 3224371200 | bytes 16777216 | tf_op jit(solution)/shard_map/rmwq,qmwk->rmk/dot_general | solution.py:77
  205.5 6.8 %fusion.19 = f32[512,4,768]{0,2,1:T(8,128)S(1)} fusion(bf16[512,4,2,512]{3,1,2,0:T(4,128)(2,1)} %all-gather.2.cloned.1.call-done, bf16[512,4,1,768]{0,3,1,2:T(8,128)(2,1)S(1)} %copy-done.6, bf16[512,4,1,768]{0,3,1,2:T(8,128)(2,1)} %get-tuple-element.12), kind=kOutput, calls=%fused_computation.32 | convolution fusion | flops 3224371200 | bytes 16777216 | tf_op jit(solution)/shard_map/rmwp,rmwk->pmk/dot_general | solution.py:80
  212.3 1.9 fusion.16
  214.7 11.7 %psum.14 = f32[2,512]{1,0:T(2,128)S(1)} all-reduce(f32[2,512]{1,0:T(2,128)S(1)} %fusion.36), channel_id=1, replica_groups=mesh['dir'=8,'freq'=4] {'freq'}, use_global_device_ids=true, to_apply=%region_2.0 | all-reduce | flops 1024 | bytes 8192 | tf_op jit(solution)/shard_map/psum | solution.py:91
  226.3 1.2 multiply_reduce_fusion
  227.5 12.5 %psum.15 = f32[]{:T(128)} all-reduce(f32[]{:T(128)} %get-tuple-element.18), channel_id=1, replica_groups=mesh['dir'=8,'freq'=4] {'dir'}, use_global_device_ids=true, to_apply=%region_4.0 | all-reduce | flops 1 | bytes 8 | tf_op jit(solution)/shard_map/psum | solution.py:93
  (54 shorter events, 9.6 us)
Async XLA Ops:
  7.2 219.2 %copy-start = (f32[512,512]{1,0:T(8,128)S(1)}, f32[512,512]{1,0:T(8,128)}, u32[]{:S(2)}) copy-start(f32[512,512]{1,0:T(8,128)} %param.13) | copy-start | bytes 3145732
  7.2 120.1 %all-reduce.3.cloned.1.call-start = ((), (), s32[]{:S(2)}) async-start(), calls=%async_computation.2 | async-start | bytes 8388608
  8.8 5.5 %copy-start.9 = (f32[2,512]{1,0:T(2,128)S(1)}, f32[2,512]{1,0:T(2,128)}, u32[]{:S(2)}) copy-start(f32[2,512]{1,0:T(2,128)} %param.12) | copy-start | bytes 12292
  8.8 5.5 %copy-start.10 = (s32[384]{0:T(512)S(1)}, s32[384]{0:T(512)}, u32[]{:S(2)}) copy-start(s32[384]{0:T(512)} %param.18) | copy-start | bytes 4612
  8.8 6.0 %copy-start.11 = (f32[2,2,512]{2,1,0:T(2,128)S(1)}, f32[2,2,512]{2,1,0:T(2,128)}, u32[]{:S(2)}) copy-start(f32[2,2,512]{2,1,0:T(2,128)} %param.14) | copy-start | bytes 24580
  8.8 6.0 %copy-start.12 = (f32[2,384]{1,0:T(2,128)S(1)}, f32[2,384]{1,0:T(2,128)}, u32[]{:S(2)}) copy-start(f32[2,384]{1,0:T(2,128)} %param.15) | copy-start | bytes 9220
  14.8 14.2 %slice-start = ((s8[6291456]{0:T(1024)(128)(4,1)}), s8[4194304]{0:T(1024)(128)(4,1)S(1)}, s32[]{:S(2)}) async-start(s8[6291456]{0:T(1024)(128)(4,1)} %bitcast.76), calls=%async_computation.3 | async-start | bytes 8388608
  14.9 14.2 %slice-start.1 = ((s8[6291456]{0:T(1024)(128)(4,1)}), s8[2097152]{0:T(1024)(128)(4,1)S(1)}, s32[]{:S(2)}) async-start(s8[6291456]{0:T(1024)(128)(4,1)} %bitcast.76), calls=%async_computation.4 | async-start | bytes 4194304
  32.3 2.4 copy-start.1
  43.6 0.9 copy-start.8
  43.6 2.4 copy-start.13
  132.7 13.1 %all-to-all-start = ((f32[8,1,16384]{2,1,0:T(1,128)}), f32[8,1,16384]{2,1,0:T(1,128)S(1)}, u32[]{:S(2)}, u32[]{:S(2)}) async-start(f32[8,1,16384]{2,1,0:T(1,128)} %reshape.106), calls=%async_computation | async-start | bytes 1048576 | tf_op jit(solution)/shard_map/all_to_all | solution.py:59
  136.2 61.6 %all-gather.2.cloned.1.call-start = ((), (), s32[]{:S(2)}) async-start(), calls=%async_computation.1 | async-start | bytes 4718592 | tf_op jit(solution)/shard_map/all_gather | solution.py:76
  145.9 0.8 copy-start.7
  158.4 0.8 copy-start.5
  161.9 5.4 %copy-start.2 = (bf16[512,4,384]{0,2,1:T(8,128)(2,1)S(1)}, bf16[512,4,384]{0,2,1:T(8,128)(2,1)}, u32[]{:S(2)}) copy-start(bf16[512,4,384]{0,2,1:T(8,128)(2,1)} %copy-done.1) | copy-start | bytes 4718596
  162.0 5.4 %copy-start.4 = (bf16[512,4,384]{0,2,1:T(8,128)(2,1)S(1)}, bf16[512,4,384]{0,2,1:T(8,128)(2,1)}, u32[]{:S(2)}) copy-start(bf16[512,4,384]{0,2,1:T(8,128)(2,1)} %get-tuple-element.4) | copy-start | bytes 4718596
  197.8 7.8 %copy-start.6 = (bf16[512,4,1,768]{0,3,1,2:T(8,128)(2,1)S(1)}, bf16[512,4,1,768]{0,3,1,2:T(8,128)(2,1)}, u32[]{:S(2)}) copy-start(bf16[512,4,1,768]{0,3,1,2:T(8,128)(2,1)} %get-tuple-element.9) | copy-start | bytes 9437188
  205.5 6.8 %copy-start.3 = (bf16[512,4,384]{0,2,1:T(8,128)(2,1)S(1)}, bf16[512,4,384]{0,2,1:T(8,128)(2,1)}, u32[]{:S(2)}) copy-start(bf16[512,4,384]{0,2,1:T(8,128)(2,1)} %copy-done.1) | copy-start | bytes 4718596
Sparse Core Ops, SparseCore 0:
  43.8 83.5 all-reduce.2
  162.1 35.6 all-gather.1
where the time goes:
time: 249 us; the launch traced here: 248 us
  waiting for transfers between devices  106 us (43%)
  matrix products  36.4 us (15%)
  local copies, waits for them, and re-layouts  34.8 us (14%)
  other arithmetic  27.3 us (11%)
  blocking collectives  24.1 us (10%)
  between operations  15.6 us (6%)
  starting transfers between devices  3.75 us (2%)
    unnamed x3, waiting for transfers between devices  80.1 us
    all_gather x1, waiting for transfers between devices, body(): rows_piece = lax.all_gather(resid_half, 'dir', axis=0, tiled=True)  18.7 us
    dot_general x1, matrix products, body(): geometry = jnp.einsum('mcp,ck->pmk', uv_each, source_lm, precision=highest)  14.2 us
    psum x1, blocking collectives, body(): total_sq = lax.psum(jnp.sum(smooth * smooth), 'dir')  12.5 us
    psum x1, blocking collectives, body(): total_grad = lax.psum(local_grad, 'freq')  11.7 us
    unnamed x36, local copies, waits for them, and re-layouts  8.85 us
    dot_general x1, matrix products, body(): jnp.einsum('rmwq,qmwk->rmk', rows_piece, forward_mat, preferred_element_t...  7.74 us
    all_to_all x1, waiting for transfers between devices, body(): lax.all_to_all(packed_rows, 'dir', split_axis=2, concat_axis=0, tiled=True)  7.36 us
  transfers between devices with their start and end apart: 3, of which 3 were waited for; matrix products, arithmetic and copies ran while one was open for 9% of the time, Pallas kernels for 0%

commit v1 on v0

--- a/solution.py
+++ b/solution.py
@@ -73,7 +73,12 @@
     conj_mat = jnp.concatenate([phasor_re, -phasor_im], axis=2)
     dual_mat = jnp.concatenate([phasor_im, phasor_re], axis=2)
     adjoint_mat = jnp.stack([conj_mat, dual_mat], axis=2)
-    rows_piece = lax.all_gather(resid_half, "dir", axis=0, tiled=True)
+    ring = [resid_half]
+    for hop in range(7):
+        ring.append(lax.ppermute(ring[-1], "dir", [(dev, (dev + 1) % 8) for dev in range(8)]))
+    rows_piece = jnp.roll(
+        jnp.concatenate(ring[::-1], axis=0), (lax.axis_index("dir") + 1) * ring[0].shape[0], axis=0
+    )
     row_part = jnp.einsum(
         "rmwq,qmwk->rmk", rows_piece, forward_mat, preferred_element_type=jnp.float32
     )

time: 249 us -> 287 us (1.15)
  waiting for transfers between devices: 106 us -> 142 us
  local copies, waits for them, and re-layouts: 34.8 us -> 41.2 us
  other arithmetic: 27.3 us -> 24 us
    ppermute x0 -> x7, waiting for transfers between devices: none -> 57 us  [body(): lax.ppermute(ring[-1], 'dir', [(dev, (dev + 1) % 8) for dev in range(8)])]
    all_gather x1 -> x0, waiting for transfers between devices: 18.7 us -> none  [body(): rows_piece = lax.all_gather(resid_half, 'dir', axis=0, tiled=True)]
    unnamed x36 -> x69, local copies, waits for them, and re-layouts: 8.85 us -> 21.3 us
    all_to_all x1, waiting for transfers between devices: 7.36 us -> 2.99 us  [body(): lax.all_to_all(packed_rows, 'dir', split_axis=2, concat_axis=0, tiled=True)]
    another operation x2, local copies, waits for them, and re-layouts: 4.08 us -> 1.08 us  [body(): jnp.stack([(packed_rows + mirrored) * 0.5, (packed_rows - mirrored) * 0.5...]
    unnamed x3 -> x2, waiting for transfers between devices: 80.1 us -> 81.9 us
  transfers between devices with their start and end apart: 3 -> 9, of which waited for: 3 -> 9; matrix products, arithmetic and copies ran while one was open for 9% -> 6% of each run, Pallas kernels for 0% -> 0%
where the time goes in v1:
time: 287 us; the launch traced here: 286 us
  waiting for transfers between devices  142 us (49%)
  local copies, waits for them, and re-layouts  41.2 us (14%)
  matrix products  34.7 us (12%)
  blocking collectives  24.1 us (8%)
  other arithmetic  24 us (8%)
  between operations  15.9 us (6%)
  starting transfers between devices  4.45 us (2%)
    unnamed x2, waiting for transfers between devices  81.9 us
    ppermute x7, waiting for transfers between devices, body(): lax.ppermute(ring[-1], 'dir', [(dev, (dev + 1) % 8) for dev in range(8)])  57 us
    unnamed x69, local copies, waits for them, and re-layouts  21.3 us
    dot_general x1, matrix products, body(): geometry = jnp.einsum('mcp,ck->pmk', uv_each, source_lm, precision=highest)  14.2 us
    psum x1, blocking collectives, body(): total_sq = lax.psum(jnp.sum(smooth * smooth), 'dir')  12.4 us
    psum x1, blocking collectives, body(): total_grad = lax.psum(local_grad, 'freq')  11.7 us
    dot_general x1, matrix products, body(): jnp.einsum('rmwp,rmwk->pmk', rows_piece, adjoint_mat, preferred_element_t...  7.47 us
  transfers between devices with their start and end apart: 9, of which 9 were waited for; matrix products, arithmetic and copies ran while one was open for 6% of the time, Pallas kernels for 0%

profile of v1, /device:TPU:0, one launch (start us, length us, event | category | flops | bytes accessed | tf_op | source)
XLA Modules:
  0.0 286.2 jit_solution(10706411373598960313)
XLA Ops:
  8.2 5.5 %copy.27 = f32[2,2,2,512,384]{3,4,1,0,2:T(8,128)} copy(bf16[2,2,2,512,384]{4,3,2,1,0:T(8,128)(2,1)} %param.17) | data formatting | bytes 9437184 | tf_op jit(solution)/shard_map/convert_element_type | solution.py:44
  14.2 14.2 %fusion.46 = (f32[512,4,384]{0,2,1:T(8,128)S(1)}, f32[512,4,384]{0,2,1:T(8,128)S(1)}) fusion(f32[4,2,512]{2,1,0:T(2,128)S(1)} %bitcast.94, f32[2,384]{1,0:T(2,128)S(1)} %copy-done.20, f32[4]{0:T(128)S(1)} %get-tuple-element.16, f32[4]{0:T(128)S(1)} %div.26, f32[512,384]{0,1:T(8,128)S(1)} %convolution_bitcast_fusion), kind=kOutput, calls=%fused_computation.85 | convolution fusion | flops 21233664 | bytes 7097376 | tf_op jit(solution)/shard_map/mcp,ck->pmk/dot_general | solution.py:39
  28.4 3.3 %fusion.45 = (bf16[512,4,384]{0,2,1:T(8,128)(2,1)}, bf16[512,4,384]{0,2,1:T(8,128)(2,1)S(1)}, bf16[512,4,1,384]{0,3,1,2:T(8,128)(2,1)}, bf16[512,4,384]{0,2,1:T(8,128)(2,1)S(1)}) fusion(f32[512,4,384]{0,2,1:T(8,128)S(1)} %get-tuple-element.10, f32[4,2,512,384]{2,3,0,1:T(8,128)S(1)} %bitcast.85, f32[512,4,384]{0,2,1:T(8,128)S(1)} %get-tuple-element.11, ...), kind=kLoop, calls=%fused_computation.84 | loop fusion | flops 9437184 | bytes 18875904 | tf_op jit(solution)/shard_map/neg | solution.py:73
  32.0 2.1 fusion.30
  34.1 3.5 %multiply_bitcast_fusion = f32[512,4,512]{0,2,1:T(8,128)} fusion(f32[4,512,512]{2,1,0:T(8,128)S(1)} %fusion.30, bf16[512,4,384]{0,2,1:T(8,128)(2,1)S(1)} %get-tuple-element.5, bf16[512,4,384]{0,2,1:T(8,128)(2,1)S(1)} %neg.16, bf16[512,4,384]{0,2,1:T(8,128)(2,1)S(1)} %get-tuple-element.7), kind=kOutput, calls=%fused_computation.8 | convolution fusion | flops 1625292800 | bytes 13107200 | tf_op jit(solution)/shard_map/pmk,qmk->pmq/dot_general | solution.py:55
  37.6 5.4 %copy.32 = f32[512,4,512]{2,1,0:T(4,128)} copy(f32[512,4,512]{0,2,1:T(8,128)} %multiply_bitcast_fusion) | data formatting | bytes 8388608 | tf_op jit(solution)/shard_map/mul | solution.py:57
  44.9 81.8 %all-reduce.3.cloned.1.call-done = f32[512,4,512]{2,1,0:T(4,128)} async-done(((f32[512,4,512]{2,1,0:T(4,128)}), f32[512,4,512]{2,1,0:T(4,128)}) %all-reduce.3.cloned.1.call-update) | async-done | bytes 4194320
  129.2 3.0 %reshape.106 = f32[8,1,16384]{2,1,0:T(1,128)} reshape(f32[512,4,64]{2,1,0:T(4,128)} %bitcast.91) | data formatting | bytes 1048576
  132.2 4.3 %all-to-all-start = ((f32[8,1,16384]{2,1,0:T(1,128)}), f32[8,1,16384]{2,1,0:T(1,128)}, u32[]{:S(2)}, u32[]{:S(2)}) async-start(f32[8,1,16384]{2,1,0:T(1,128)} %reshape.106), calls=%async_computation | async-start | bytes 1048576 | tf_op jit(solution)/shard_map/all_to_all | solution.py:59
  138.3 2.9 copy.40
  143.1 3.0 %all-to-all-done = f32[8,1,16384]{2,1,0:T(1,128)} async-done(((f32[8,1,16384]{2,1,0:T(1,128)}), f32[8,1,16384]{2,1,0:T(1,128)}, u32[]{:S(2)}, u32[]{:S(2)}) %all-to-all-start) | async-done | bytes 524320 | tf_op jit(solution)/shard_map/all_to_all | solution.py:59
  146.6 3.7 %reduce = f32[8,16384]{1,0:T(8,128)} reduce(f32[8,1,16384]{2,1,0:T(1,128)} %all-to-all-done, f32[]{:T(128)} %broadcast.61), dimensions={1}, to_apply=%all_to_all.13.reduce_sub_computation | reduce | bytes 1048580 | tf_op jit(solution)/shard_map/all_to_all | solution.py:59
  150.3 2.7 reshape.107
  153.0 2.8 copy.63
  155.8 2.3 all_to_all.16
  159.4 2.0 fusion.33
  161.5 9.5 %collective-permute-done = bf16[64,4,2,512]{3,0,2,1:T(8,128)(2,1)S(1)} collective-permute-done((bf16[64,4,2,512]{3,0,2,1:T(8,128)(2,1)S(1)}, bf16[64,4,2,512]{3,0,2,1:T(8,128)(2,1)S(1)}, u32[]{:S(2)}, u32[]{:S(2)}) %collective-permute-start) | collective-permute-done | bytes 524320 | tf_op jit(solution)/shard_map/ppermute | solution.py:78
  171.0 9.5 %collective-permute-done.1 = bf16[64,4,2,512]{3,0,2,1:T(8,128)(2,1)S(1)} collective-permute-done((bf16[64,4,2,512]{3,0,2,1:T(8,128)(2,1)S(1)}, bf16[64,4,2,512]{3,0,2,1:T(8,128)(2,1)S(1)}, u32[]{:S(2)}, u32[]{:S(2)}) %collective-permute-start.1) | collective-permute-done | bytes 524320 | tf_op jit(solution)/shard_map/ppermute | solution.py:78
  181.3 8.7 %collective-permute-done.2 = bf16[64,4,2,512]{3,0,2,1:T(8,128)(2,1)S(1)} collective-permute-done((bf16[64,4,2,512]{3,0,2,1:T(8,128)(2,1)S(1)}, bf16[64,4,2,512]{3,0,2,1:T(8,128)(2,1)S(1)}, u32[]{:S(2)}, u32[]{:S(2)}) %collective-permute-start.2) | collective-permute-done | bytes 524320 | tf_op jit(solution)/shard_map/ppermute | solution.py:78
  190.8 9.6 %collective-permute-done.3 = bf16[64,4,2,512]{3,0,2,1:T(8,128)(2,1)} collective-permute-done((bf16[64,4,2,512]{3,0,2,1:T(8,128)(2,1)S(1)}, bf16[64,4,2,512]{3,0,2,1:T(8,128)(2,1)}, u32[]{:S(2)}, u32[]{:S(2)}) %collective-permute-start.3) | collective-permute-done | bytes 524320 | tf_op jit(solution)/shard_map/ppermute | solution.py:78
  200.4 9.8 %collective-permute-done.4 = bf16[64,4,2,512]{3,0,2,1:T(8,128)(2,1)} collective-permute-done((bf16[64,4,2,512]{3,0,2,1:T(8,128)(2,1)}, bf16[64,4,2,512]{3,0,2,1:T(8,128)(2,1)}, u32[]{:S(2)}, u32[]{:S(2)}) %collective-permute-start.4) | collective-permute-done | bytes 524320 | tf_op jit(solution)/shard_map/ppermute | solution.py:78
  210.2 2.5 maximum_negate_fusion
  212.8 3.1 %fusion.29 = (bf16[512,4,1,768]{0,3,1,2:T(8,128)(2,1)S(1)}, bf16[512,4,1,768]{0,3,1,2:T(8,128)(2,1)}, bf16[512,4,1,768]{0,3,1,2:T(8,128)(2,1)}) fusion(bf16[512,4,384]{0,2,1:T(8,128)(2,1)S(1)} %copy-done.2, bf16[512,4,384]{0,2,1:T(8,128)(2,1)S(1)} %get-tuple-element.7, bf16[512,4,384]{0,2,1:T(8,128)(2,1)S(1)} %copy-done.3), kind=kLoop, calls=%fused_computation.34 | loop fusion | flops 17301504 | bytes 14155776 | tf_op jit(solution)/shard_map/stack | solution.py:72
  215.9 4.0 %collective-permute-done.5 = bf16[64,4,2,512]{3,0,2,1:T(8,128)(2,1)S(1)} collective-permute-done((bf16[64,4,2,512]{3,0,2,1:T(8,128)(2,1)}, bf16[64,4,2,512]{3,0,2,1:T(8,128)(2,1)S(1)}, u32[]{:S(2)}, u32[]{:S(2)}) %collective-permute-start.5) | collective-permute-done | bytes 524320 | tf_op jit(solution)/shard_map/ppermute | solution.py:78
  221.3 2.3 fusion.31
  223.6 5.9 %collective-permute-done.6 = bf16[64,4,2,512]{3,0,2,1:T(8,128)(2,1)S(1)} collective-permute-done((bf16[64,4,2,512]{3,0,2,1:T(8,128)(2,1)S(1)}, bf16[64,4,2,512]{3,0,2,1:T(8,128)(2,1)S(1)}, u32[]{:S(2)}, u32[]{:S(2)}) %collective-permute-start.6) | collective-permute-done | bytes 524320 | tf_op jit(solution)/shard_map/ppermute | solution.py:78
  234.5 3.3 %copy-done.15 = bf16[1024,4,2,512]{3,0,2,1:T(8,128)(2,1)} copy-done((bf16[1024,4,2,512]{3,0,2,1:T(8,128)(2,1)}, bf16[1024,4,2,512]{3,0,2,1:T(8,128)(2,1)S(1)}, u32[]{:S(2)}) %copy-start.15) | copy-done | bytes 8388632
  237.7 5.3 %fusion.24 = f32[512,4,768]{0,2,1:T(8,128)S(1)} fusion(bf16[512,4,1,768]{0,3,1,2:T(8,128)(2,1)S(1)} %maximum_negate_fusion, bf16[512,4,1,768]{0,3,1,2:T(8,128)(2,1)S(1)} %get-tuple-element.8, bf16[1024,4,2,512]{3,0,2,1:T(8,128)(2,1)} %copy-done.15, s32[]{:T(128)S(6)} %select_n.14), kind=kOutput, calls=%fused_computation.33 | convolution fusion | flops 3224371200 | bytes 16777220 | tf_op jit(solution)/shard_map/rmwq,qmwk->rmk/dot_general | solution.py:82
  243.0 7.5 %fusion.19 = f32[512,4,768]{0,2,1:T(8,128)S(1)} fusion(bf16[512,4,1,768]{0,3,1,2:T(8,128)(2,1)} %get-tuple-element.9, bf16[512,4,1,768]{0,3,1,2:T(8,128)(2,1)} %get-tuple-element.12, bf16[1024,4,2,512]{3,0,2,1:T(8,128)(2,1)} %copy-done.15, s32[]{:T(128)S(6)} %select_n.14), kind=kOutput, calls=%fused_computation.32 | convolution fusion | flops 3224371200 | bytes 16777220 | tf_op jit(solution)/shard_map/rmwp,rmwk->pmk/dot_general | solution.py:85
  250.5 1.9 fusion.16
  252.8 11.7 %psum.14 = f32[2,512]{1,0:T(2,128)S(1)} all-reduce(f32[2,512]{1,0:T(2,128)S(1)} %fusion.36), channel_id=1, replica_groups=mesh['dir'=8,'freq'=4] {'freq'}, use_global_device_ids=true, to_apply=%region_2.3 | all-reduce | flops 1024 | bytes 8192 | tf_op jit(solution)/shard_map/psum | solution.py:96
  265.7 12.4 %psum.15 = f32[]{:T(128)} all-reduce(f32[]{:T(128)} %get-tuple-element.18), channel_id=1, replica_groups=mesh['dir'=8,'freq'=4] {'dir'}, use_global_device_ids=true, to_apply=%region_4.5 | all-reduce | flops 1 | bytes 8 | tf_op jit(solution)/shard_map/psum | solution.py:98
  (96 shorter events, 21.0 us)
Async XLA Ops:
  7.2 257.3 %copy-start = (f32[512,512]{1,0:T(8,128)S(1)}, f32[512,512]{1,0:T(8,128)}, u32[]{:S(2)}) copy-start(f32[512,512]{1,0:T(8,128)} %param.13) | copy-start | bytes 3145732
  7.2 119.6 %all-reduce.3.cloned.1.call-start = ((), (), s32[]{:S(2)}) async-start(), calls=%async_computation.1 | async-start | bytes 8388608
  8.1 5.5 %copy-start.19 = (f32[384]{0:T(512)S(1)}, f32[384]{0:T(512)}, u32[]{:S(2)}) copy-start(f32[384]{0:T(512)} %param.16) | copy-start | bytes 4612
  8.1 5.5 %copy-start.16 = (f32[2,512]{1,0:T(2,128)S(1)}, f32[2,512]{1,0:T(2,128)}, u32[]{:S(2)}) copy-start(f32[2,512]{1,0:T(2,128)} %param.12) | copy-start | bytes 12292
  8.1 5.5 %copy-start.17 = (s32[384]{0:T(512)S(1)}, s32[384]{0:T(512)}, u32[]{:S(2)}) copy-start(s32[384]{0:T(512)} %param.18) | copy-start | bytes 4612
  8.1 6.1 %copy-start.18 = (f32[2,2,512]{2,1,0:T(2,128)S(1)}, f32[2,2,512]{2,1,0:T(2,128)}, u32[]{:S(2)}) copy-start(f32[2,2,512]{2,1,0:T(2,128)} %param.14) | copy-start | bytes 24580
  8.1 6.1 %copy-start.20 = (f32[2,384]{1,0:T(2,128)S(1)}, f32[2,384]{1,0:T(2,128)}, u32[]{:S(2)}) copy-start(f32[2,384]{1,0:T(2,128)} %param.15) | copy-start | bytes 9220
  14.2 14.2 %slice-start = ((s8[6291456]{0:T(1024)(128)(4,1)}), s8[4194304]{0:T(1024)(128)(4,1)S(1)}, s32[]{:S(2)}) async-start(s8[6291456]{0:T(1024)(128)(4,1)} %bitcast.83), calls=%async_computation.2 | async-start | bytes 8388608
  14.2 14.2 %slice-start.1 = ((s8[6291456]{0:T(1024)(128)(4,1)}), s8[2097152]{0:T(1024)(128)(4,1)S(1)}, s32[]{:S(2)}) async-start(s8[6291456]{0:T(1024)(128)(4,1)} %bitcast.83), calls=%async_computation.3 | async-start | bytes 4194304
  31.7 2.4 copy-start.1
  132.2 13.9 %all-to-all-start = ((f32[8,1,16384]{2,1,0:T(1,128)}), f32[8,1,16384]{2,1,0:T(1,128)}, u32[]{:S(2)}, u32[]{:S(2)}) async-start(f32[8,1,16384]{2,1,0:T(1,128)} %reshape.106), calls=%async_computation | async-start | bytes 1048576 | tf_op jit(solution)/shard_map/all_to_all | solution.py:59
  159.3 11.6 %copy-start.4 = (f32[64,4,512]{2,0,1:T(8,128)}, f32[64,4,512]{2,0,1:T(8,128)S(1)}, u32[]{:S(2)}) copy-start(f32[64,4,512]{2,0,1:T(8,128)S(1)} %get-tuple-element.14) | copy-start | bytes 1572868
  159.4 11.6 %copy-start.6 = (f32[64,4,512]{2,0,1:T(8,128)}, f32[64,4,512]{2,0,1:T(8,128)S(1)}, u32[]{:S(2)}) copy-start(f32[64,4,512]{2,0,1:T(8,128)S(1)} %get-tuple-element.13) | copy-start | bytes 1572868
  161.4 9.6 %collective-permute-start = (bf16[64,4,2,512]{3,0,2,1:T(8,128)(2,1)S(1)}, bf16[64,4,2,512]{3,0,2,1:T(8,128)(2,1)S(1)}, u32[]{:S(2)}, u32[]{:S(2)}) collective-permute-start(bf16[64,4,2,512]{3,0,2,1:T(8,128)(2,1)S(1)} %fusion.33), channel_id=1, source_target_pairs={{0,4},{4,8},{8,12},{12,16},{16,20},{20,24},{24,28},{28,0},{1,5},{5... | collective-permute-start | bytes 1572872 | tf_op jit(solution)/shard_map/ppermute | solution.py:78
  171.0 9.5 %copy-start.9 = (bf16[64,4,2,512]{3,0,2,1:T(8,128)(2,1)}, bf16[64,4,2,512]{3,0,2,1:T(8,128)(2,1)S(1)}, u32[]{:S(2)}) copy-start(bf16[64,4,2,512]{3,0,2,1:T(8,128)(2,1)S(1)} %collective-permute-done) | copy-start | bytes 1572868
  171.0 9.5 %collective-permute-start.1 = (bf16[64,4,2,512]{3,0,2,1:T(8,128)(2,1)S(1)}, bf16[64,4,2,512]{3,0,2,1:T(8,128)(2,1)S(1)}, u32[]{:S(2)}, u32[]{:S(2)}) collective-permute-start(bf16[64,4,2,512]{3,0,2,1:T(8,128)(2,1)S(1)} %collective-permute-done), channel_id=1, source_target_pairs={{0,4},{4,8},{8,12},{12,16},{16,20},{20,24},{24,28},{28,0},{1,5},{5... | collective-permute-start | bytes 1572872 | tf_op jit(solution)/shard_map/ppermute | solution.py:78
  180.5 0.8 copy-start.11
  180.5 9.5 %collective-permute-start.2 = (bf16[64,4,2,512]{3,0,2,1:T(8,128)(2,1)S(1)}, bf16[64,4,2,512]{3,0,2,1:T(8,128)(2,1)S(1)}, u32[]{:S(2)}, u32[]{:S(2)}) collective-permute-start(bf16[64,4,2,512]{3,0,2,1:T(8,128)(2,1)S(1)} %collective-permute-done.1), channel_id=1, source_target_pairs={{0,4},{4,8},{8,12},{12,16},{16,20},{20,24},{24,28},{28,0},{1,5},{5... | collective-permute-start | bytes 1572872 | tf_op jit(solution)/shard_map/ppermute | solution.py:78
  190.0 0.8 copy-start.13
  190.8 9.6 %collective-permute-start.3 = (bf16[64,4,2,512]{3,0,2,1:T(8,128)(2,1)S(1)}, bf16[64,4,2,512]{3,0,2,1:T(8,128)(2,1)}, u32[]{:S(2)}, u32[]{:S(2)}) collective-permute-start(bf16[64,4,2,512]{3,0,2,1:T(8,128)(2,1)S(1)} %collective-permute-done.2), channel_id=1, source_target_pairs={{0,4},{4,8},{8,12},{12,16},{16,20},{20,24},{24,28},{28,0},{1,5},{5... | collective-permute-start | bytes 1572872 | tf_op jit(solution)/shard_map/ppermute | solution.py:78
  200.4 9.8 %collective-permute-start.4 = (bf16[64,4,2,512]{3,0,2,1:T(8,128)(2,1)}, bf16[64,4,2,512]{3,0,2,1:T(8,128)(2,1)}, u32[]{:S(2)}, u32[]{:S(2)}) collective-permute-start(bf16[64,4,2,512]{3,0,2,1:T(8,128)(2,1)} %collective-permute-done.3), channel_id=1, source_target_pairs={{0,4},{4,8},{8,12},{12,16},{16,20},{20,24},{24,28},{28,0},{1,5},{5... | collective-permute-start | bytes 1572872 | tf_op jit(solution)/shard_map/ppermute | solution.py:78
  200.4 12.3 %copy-start.2 = (bf16[512,4,384]{0,2,1:T(8,128)(2,1)S(1)}, bf16[512,4,384]{0,2,1:T(8,128)(2,1)}, u32[]{:S(2)}) copy-start(bf16[512,4,384]{0,2,1:T(8,128)(2,1)} %copy-done.1) | copy-start | bytes 4718596
  200.4 12.4 %copy-start.3 = (bf16[512,4,384]{0,2,1:T(8,128)(2,1)S(1)}, bf16[512,4,384]{0,2,1:T(8,128)(2,1)}, u32[]{:S(2)}) copy-start(bf16[512,4,384]{0,2,1:T(8,128)(2,1)} %get-tuple-element.4) | copy-start | bytes 4718596
  210.2 9.7 %collective-permute-start.5 = (bf16[64,4,2,512]{3,0,2,1:T(8,128)(2,1)}, bf16[64,4,2,512]{3,0,2,1:T(8,128)(2,1)S(1)}, u32[]{:S(2)}, u32[]{:S(2)}) collective-permute-start(bf16[64,4,2,512]{3,0,2,1:T(8,128)(2,1)} %collective-permute-done.4), channel_id=1, source_target_pairs={{0,4},{4,8},{8,12},{12,16},{16,20},{20,24},{24,28},{28,0},{1,5},{5... | collective-permute-start | bytes 1572872 | tf_op jit(solution)/shard_map/ppermute | solution.py:78
  212.8 7.4 %copy-start.7 = (f32[64,4,512]{2,0,1:T(8,128)S(1)}, f32[64,4,512]{2,0,1:T(8,128)}, u32[]{:S(2)}) copy-start(f32[64,4,512]{2,0,1:T(8,128)} %copy-done.6) | copy-start | bytes 1572868
  212.8 7.9 %copy-start.5 = (f32[64,4,512]{2,0,1:T(8,128)S(1)}, f32[64,4,512]{2,0,1:T(8,128)}, u32[]{:S(2)}) copy-start(f32[64,4,512]{2,0,1:T(8,128)} %copy-done.4) | copy-start | bytes 1572868
  212.8 8.5 %copy-start.8 = (f32[64,2,2,2,512]{4,3,2,1,0:T(2,128)S(1)}, f32[64,2,2,2,512]{4,3,2,1,0:T(2,128)}, u32[]{:S(2)}) copy-start(f32[64,2,2,2,512]{4,3,2,1,0:T(2,128)} %param.10) | copy-start | bytes 3145732
  219.9 9.5 %collective-permute-start.6 = (bf16[64,4,2,512]{3,0,2,1:T(8,128)(2,1)S(1)}, bf16[64,4,2,512]{3,0,2,1:T(8,128)(2,1)S(1)}, u32[]{:S(2)}, u32[]{:S(2)}) collective-permute-start(bf16[64,4,2,512]{3,0,2,1:T(8,128)(2,1)S(1)} %collective-permute-done.5), channel_id=1, source_target_pairs={{0,4},{4,8},{8,12},{12,16},{16,20},{20,24},{24,28},{28,0},{1,5},{5... | collective-permute-start | bytes 1572872 | tf_op jit(solution)/shard_map/ppermute | solution.py:78
  221.3 10.5 %copy-start.14 = (bf16[64,4,2,512]{3,0,2,1:T(8,128)(2,1)S(1)}, bf16[64,4,2,512]{3,0,2,1:T(8,128)(2,1)}, u32[]{:S(2)}) copy-start(bf16[64,4,2,512]{3,0,2,1:T(8,128)(2,1)} %copy-done.13) | copy-start | bytes 1572868
  221.3 10.5 %copy-start.12 = (bf16[64,4,2,512]{3,0,2,1:T(8,128)(2,1)S(1)}, bf16[64,4,2,512]{3,0,2,1:T(8,128)(2,1)}, u32[]{:S(2)}) copy-start(bf16[64,4,2,512]{3,0,2,1:T(8,128)(2,1)} %copy-done.11) | copy-start | bytes 1572868
  221.3 10.6 %copy-start.10 = (bf16[64,4,2,512]{3,0,2,1:T(8,128)(2,1)S(1)}, bf16[64,4,2,512]{3,0,2,1:T(8,128)(2,1)}, u32[]{:S(2)}) copy-start(bf16[64,4,2,512]{3,0,2,1:T(8,128)(2,1)} %copy-done.9) | copy-start | bytes 1572868
  234.4 3.3 %copy-start.15 = (bf16[1024,4,2,512]{3,0,2,1:T(8,128)(2,1)}, bf16[1024,4,2,512]{3,0,2,1:T(8,128)(2,1)S(1)}, u32[]{:S(2)}) copy-start(bf16[1024,4,2,512]{3,0,2,1:T(8,128)(2,1)S(1)} %constant_dynamic-update-slice_fusion) | copy-start | bytes 25165828
  (1 other events, 0.7 us)
Sparse Core Ops, SparseCore 0:
  43.2 83.5 all-reduce.2
